TPU v7x, 32 devices: a whole 2x2x4 slice. The times are simulated.
32 devices in a mesh: groups: 2 (over y), blk: 4 (over z), heads: 2 (over x), rows: 2 (over core).
Axes of the slice: x: 2, y: 2, z: 4, core: 2. Of those that a mesh axis runs over, the one named last changes fastest.
Arguments:
- queries: bfloat16 [64, 16, 256], P(('groups', 'blk', 'rows'), 'heads'), parts along dimension 0, may hold values from -128 to 128
- src_keys: bfloat16 [12288, 8, 256], P(('groups', 'blk'), 'heads'), parts along dimension 0, may hold values from -6 to 6
- src_values: bfloat16 [12288, 8, 256], P(('groups', 'blk'), 'heads'), parts along dimension 0, may hold values from -6 to 6
- dec_state: bfloat16 [64, 3584], P('groups', ('blk', 'rows')), parts along dimension 0, may hold values from -0.59765625 to 0.59765625
- mask_embed: bfloat16 [3584], P(('blk', 'rows')), may hold values from -1.796875 to 1.796875
- out_weight: bfloat16 [4096, 3584], P('heads', ('blk', 'rows')), may hold values from -0.09375 to 0.09375
- norm_gain: bfloat16 [3584], P(('blk', 'rows')), may hold values from 0.5 to 1.5
- gate_weight: bfloat16 [3584, 14336], P('heads', ('blk', 'rows')), may hold values from -0.09375 to 0.09375
- up_weight: bfloat16 [3584, 14336], P('heads', ('blk', 'rows')), may hold values from -0.09375 to 0.09375
- down_weight: bfloat16 [14336, 3584], P(('blk', 'rows'), 'heads'), may hold values from -0.046875 to 0.046875
- cand_lengths: int32 [2], P('groups'), parts along dimension 0, may hold values from 64 to 128
- masked_pos: int32 [2, 48], P('groups'), parts along dimension 0, may hold values from 0 to 127, as said below
Outputs:
- stream: bfloat16 [64, 3584], P('groups', ('blk', 'rows')), parts along dimension 0
- branch: bfloat16 [64, 3584], P(('groups', 'blk', 'rows'), 'heads'), parts along dimension 0
There are 2 independent parts, one for each index of `groups`. A program takes and returns all parts, laid end to end along the dimension named above; an argument that names none is the same for every part. Nothing has to cross between parts.
Inputs may be any that keep to these rules, and one draw needn't show every extreme that they name: `masked_pos`: the 48 positions of one candidate are distinct.
All inputs are finite; a program needn't handle non-finite values.
Results may differ from a plain program's by a relative error of at most 0.03.
Values may be sent and summed in bfloat16 or wider, within the bound.
A program may use at most 64 MiB of HBM per device.

v0:
```python
import jax
import jax.numpy as jnp
from jax import lax
from jax.sharding import PartitionSpec as P

D = 3584
LEN = 128


def token_masks(cand_lengths, masked_pos, tokens):
    positions = jnp.arange(tokens, dtype=jnp.int32) % LEN
    length_tok = jnp.repeat(cand_lengths, LEN)[:tokens]
    valid_tok = positions < length_tok
    slots = jnp.arange(LEN, dtype=jnp.int32)
    masked_tok = jnp.any(masked_pos[:, :, None] == slots[None, None, :], axis=1).reshape(-1)[
        :tokens
    ]
    return (valid_tok, masked_tok)


def shards(
    queries,
    src_keys,
    src_values,
    dec_state,
    mask_embed,
    out_weight,
    norm_gain,
    gate_weight,
    up_weight,
    down_weight,
    cand_lengths,
    masked_pos,
):
    tok_dev, local_heads, head_size = queries.shape
    kv_local = src_keys.shape[1]
    group_size = local_heads // kv_local
    score_scale = head_size ** (-0.5)
    queries_all = lax.all_gather(queries, "blk", axis=0, tiled=True)
    gathered_rows = queries_all.shape[0]
    grouped = queries_all.reshape(gathered_rows, kv_local, group_size, head_size)
    scores = (
        jnp.einsum("tgjd,kgd->tgjk", grouped, src_keys, preferred_element_type=jnp.float32)
        * score_scale
    )
    local_peak = jnp.max(scores, axis=3)
    weights = jnp.exp(scores - local_peak[..., None])
    totals = jnp.sum(weights, axis=3)
    numerator = jnp.einsum(
        "tgjk,kgd->tgjd",
        weights.astype(jnp.bfloat16),
        src_values,
        preferred_element_type=jnp.float32,
    )
    highest = lax.pmax(local_peak, "blk")
    factor = jnp.exp(local_peak - highest)
    numer_own, totals_own = (
        lax.psum_scatter(
            (numerator * factor[..., None]).astype(jnp.bfloat16),
            "blk",
            scatter_dimension=0,
            tiled=True,
        ).astype(jnp.float32),
        lax.psum_scatter(
            (totals * factor).astype(jnp.bfloat16), "blk", scatter_dimension=0, tiled=True
        ).astype(jnp.float32),
    )
    attn_own = (
        (numer_own / totals_own[..., None])
        .astype(jnp.bfloat16)
        .reshape(tok_dev, local_heads * head_size)
    )
    attn_all = lax.all_gather(attn_own, ("blk", "rows"), axis=0, tiled=True)
    tokens = attn_all.shape[0]
    projected = lax.psum(
        jnp.dot(attn_all, out_weight, preferred_element_type=jnp.float32).astype(jnp.bfloat16),
        "heads",
    ).astype(jnp.float32)
    valid_tok, masked_tok = token_masks(cand_lengths, masked_pos, tokens)
    base_state = jnp.where(masked_tok[:, None], mask_embed[None, :], dec_state).astype(jnp.float32)
    stream_mid = base_state + projected
    squares = lax.psum(jnp.sum(stream_mid * stream_mid, axis=1), ("blk", "rows"))
    inv_rms = lax.rsqrt(squares / D + 1e-06)[:, None]
    normed = (stream_mid * inv_rms * norm_gain.astype(jnp.float32)).astype(jnp.bfloat16)
    keep_mask = valid_tok.astype(jnp.float32)[:, None]
    stream = (stream_mid * keep_mask).astype(jnp.bfloat16)
    normed_full = lax.all_gather(normed, ("blk", "rows"), axis=1, tiled=True)
    feature_width = gate_weight.shape[0]
    column_block = lax.dynamic_slice_in_dim(
        normed_full, lax.axis_index("heads") * feature_width, feature_width, 1
    )
    gate_part = jnp.dot(column_block, gate_weight, preferred_element_type=jnp.float32)
    up_part = jnp.dot(column_block, up_weight, preferred_element_type=jnp.float32)
    gate_rows, up_rows = (
        lax.psum(gate_part.astype(jnp.bfloat16), "heads").astype(jnp.float32),
        lax.psum(up_part.astype(jnp.bfloat16), "heads").astype(jnp.float32),
    )
    hidden = (jax.nn.gelu(gate_rows, approximate=True) * up_rows).astype(jnp.bfloat16)
    down_out = lax.psum_scatter(
        jnp.dot(hidden, down_weight, preferred_element_type=jnp.float32),
        ("blk", "rows"),
        scatter_dimension=0,
        tiled=True,
    )
    own_start = (lax.axis_index("blk") * lax.axis_size("rows") + lax.axis_index("rows")) * tok_dev
    keep_own = lax.dynamic_slice_in_dim(keep_mask, own_start, tok_dev, 0)
    return (stream, (down_out * keep_own).astype(jnp.bfloat16))


def solution(mesh):
    placed = (
        P(("groups", "blk", "rows"), "heads", None),
        P(("groups", "blk"), "heads", None),
        P(("groups", "blk"), "heads", None),
        P("groups", ("blk", "rows")),
        P(("blk", "rows")),
        P("heads", ("blk", "rows")),
        P(("blk", "rows")),
        P("heads", ("blk", "rows")),
        P("heads", ("blk", "rows")),
        P(("blk", "rows"), "heads"),
        P("groups"),
        P("groups", None),
    )
    return jax.shard_map(
        shards,
        mesh=mesh,
        in_specs=placed,
        out_specs=(P("groups", ("blk", "rows")), P(("groups", "blk", "rows"), "heads")),
        check_vma=False,
    )
```

profile of v0, /device:TPU:0, one launch (start us, length us, event | category | flops | bytes accessed | tf_op | source)
XLA Modules:
  0.0 225.8 jit_solution(5355824614726427684)
XLA Ops:
  7.2 15.3 %all_gather.9 = bf16[16,8,256]{2,1,0:T(8,128)(2,1)S(1)} all-gather(bf16[4,8,256]{2,1,0:T(8,128)(2,1)} %param.12), channel_id=1, replica_groups=mesh['groups'=2,'blk'=4,'heads'=2,'rows'=2] {'blk'}, dimensions={0}, use_global_device_ids=true | all-gather | bytes 81920 | tf_op jit(solution)/shard_map/all_gather | solution.py:39
  22.5 3.8 %fusion.48 = (f32[16,4,2]{0,2,1:T(2,128)S(1)}, f32[16,4,2,1536]{3,0,2,1:T(8,128)}) fusion(bf16[16,4,2,256]{3,0,2,1:T(8,128)(2,1)S(1)} %bitcast.36, bf16[1536,4,256,1]{2,1,0,3:T(4,128)(2,1)} %bitcast.37), kind=kOutput, calls=%fused_computation.59 | convolution fusion | flops 101056384 | bytes 3998208 | tf_op jit(solution)/shard_map/tgjd,kgd->tgjk/dot_general | solution.py:43
  26.3 11.8 %pmax.7 = f32[16,4,2]{0,2,1:T(2,128)S(1)} all-reduce(f32[16,4,2]{0,2,1:T(2,128)S(1)} %get-tuple-element.8), channel_id=1, replica_groups=mesh['groups'=2,'blk'=4,'heads'=2,'rows'=2] {'blk'}, use_global_device_ids=true, to_apply=%region_2.0 | all-reduce | flops 128 | bytes 1024 | tf_op jit(solution)/shard_map/pmax | solution.py:55
  38.2 1.4 fusion.19
  39.6 2.5 %fusion.16 = bf16[16,4,2,256]{3,0,2,1:T(8,128)(2,1)} fusion(bf16[1536,4,256,1]{2,1,0,3:T(4,128)(2,1)S(1)} %bitcast.34, f32[16,4,2,1536]{3,0,2,1:T(8,128)} %get-tuple-element.9, f32[16,4,2]{0,2,1:T(2,128)S(1)} %get-tuple-element.8, f32[16,4,2]{0,2,1:T(2,128)S(1)} %get-tuple-element.5), kind=kOutput, calls=%fused_computation.10 | convolution fusion | flops 101122048 | bytes 3998720 | tf_op jit(solution)/shard_map/tgjk,kgd->tgjd/dot_general | solution.py:49
  42.2 8.4 %all-reduce.1 = bf16[16,4,2]{0,2,1:T(2,128)(2,1)S(1)} all-reduce(bf16[16,4,2]{0,2,1:T(2,128)(2,1)S(1)} %get-tuple-element.4), channel_id=3, replica_groups=mesh['groups'=2,'blk'=4,'heads'=2,'rows'=2] {'blk'}, use_global_device_ids=true, to_apply=%region_5.0.clone | all-reduce | flops 128 | bytes 512
  51.4 0.6 dynamic-slice.5
  52.7 22.2 %all-reduce.8.cloned.1.call-done = bf16[16,4,2,256]{3,0,2,1:T(8,128)(2,1)} async-done(((bf16[16,4,2,256]{3,0,2,1:T(8,128)(2,1)}), bf16[16,4,2,256]{3,0,2,1:T(8,128)(2,1)}) %all-reduce.8.cloned.1.call-update) | async-done | bytes 65552
  74.8 0.8 fusion.39
  75.7 14.0 %all-gather = bf16[8,4,2048]{2,1,0:T(4,128)(2,1)S(1)} all-gather(bf16[1,4,2048]{2,1,0:T(4,128)(2,1)S(1)} %bitcast.35), channel_id=1, replica_groups=mesh['groups'=2,'blk'=4,'heads'=2,'rows'=2] {'blk','rows'}, dimensions={0}, use_global_device_ids=true | all-gather | bytes 147456 | tf_op jit(solution)/shard_map/all_gather | solution.py:73
  89.7 2.1 convolution_convert_fusion.2
  91.8 8.3 %psum.28 = bf16[32,448]{1,0:T(8,128)(2,1)S(1)} all-reduce(bf16[32,448]{1,0:T(8,128)(2,1)S(1)} %convolution_convert_fusion.2), channel_id=1, replica_groups=mesh['groups'=2,'blk'=4,'heads'=2,'rows'=2] {'heads'}, use_global_device_ids=true, to_apply=%region_6.7 | all-reduce | flops 14336 | bytes 57344 | tf_op jit(solution)/shard_map/psum | solution.py:75
  100.1 0.2 multiply_reduce_fusion
  100.3 13.6 %psum.29 = f32[32]{0:T(128)S(1)} all-reduce(f32[32]{0:T(128)S(1)} %multiply_reduce_fusion), channel_id=1, replica_groups=mesh['groups'=2,'blk'=4,'heads'=2,'rows'=2] {'blk','rows'}, use_global_device_ids=true, to_apply=%region_8.9 | all-reduce | flops 32 | bytes 256 | tf_op jit(solution)/shard_map/psum | solution.py:82
  114.0 0.7 fusion.38
  114.7 14.2 %all-gather.1 = bf16[8,448,32]{1,2,0:T(8,128)(2,1)S(1)} all-gather(bf16[1,448,32]{1,2,0:T(8,128)(2,1)S(1)} %get-tuple-element.6), channel_id=1, replica_groups=mesh['groups'=2,'blk'=4,'heads'=2,'rows'=2] {'blk','rows'}, dimensions={0}, use_global_device_ids=true | all-gather | bytes 258048 | tf_op jit(solution)/shard_map/all_gather | solution.py:87
  129.0 0.9 reshape.80
  130.0 4.8 %convolution_convert_fusion = bf16[32,1792]{1,0:T(8,128)(2,1)} fusion(bf16[1792,1792]{1,0:T(8,128)(2,1)} %param.20, bf16[3584,32]{0,1:T(8,128)(2,1)} %reshape.80, s32[]{:T(128)S(6)} %select_n.23), kind=kOutput, calls=%fused_computation.6 | convolution fusion | flops 205578240 | bytes 6651908 | tf_op jit(solution)/shard_map/dot_general | solution.py:93
  134.8 4.7 %convolution_convert_fusion.1 = bf16[32,1792]{1,0:T(8,128)(2,1)} fusion(bf16[1792,1792]{1,0:T(8,128)(2,1)} %param.19, bf16[3584,32]{0,1:T(8,128)(2,1)S(1)} %copy-done.1, s32[]{:T(128)S(6)} %select_n.23), kind=kOutput, calls=%fused_computation.7 | convolution fusion | flops 205578240 | bytes 6651908 | tf_op jit(solution)/shard_map/dot_general | solution.py:92
  139.6 20.3 %all-reduce.12.cloned.1.call-done = (bf16[32,1792]{1,0:T(8,128)(2,1)}, bf16[32,1792]{1,0:T(8,128)(2,1)}) async-done(((bf16[32,1792]{1,0:T(8,128)(2,1)}, bf16[32,1792]{1,0:T(8,128)(2,1)}), (bf16[32,1792]{1,0:T(8,128)(2,1)}, bf16[32,1792]{1,0:T(8,128)(2,1)})) %all-reduce.12.cloned.1.call-update) | async-done | bytes 229392 | tf_op jit(solution)/shard_map/psum | solution.py:95
  159.8 4.7 %fusion.30 = f32[32,1792]{1,0:T(8,128)} fusion(bf16[1792,1792]{1,0:T(8,128)(2,1)} %param.21, bf16[32,1792]{1,0:T(8,128)(2,1)} %get-tuple-element.2, bf16[32,1792]{1,0:T(8,128)(2,1)} %get-tuple-element.3), kind=kOutput, calls=%fused_computation.27 | convolution fusion | flops 206209024 | bytes 6881280 | tf_op jit(solution)/shard_map/dot_general | solution.py:100
  164.7 0.6 dynamic-slice.9
  165.9 51.9 %all-reduce.10.cloned.1.call-done = f32[32,1792]{1,0:T(8,128)} async-done(((f32[32,1792]{1,0:T(8,128)}), f32[32,1792]{1,0:T(8,128)}) %all-reduce.10.cloned.1.call-update) | async-done | bytes 229392
  217.8 1.5 fusion.40
  (33 shorter events, 0.7 us)
Async XLA Ops:
  7.2 32.4 %copy-start = (bf16[1536,4,256]{2,1,0:T(4,128)(2,1)S(1)}, bf16[1536,4,256]{2,1,0:T(4,128)(2,1)}, u32[]{:S(2)}) copy-start(bf16[1536,4,256]{2,1,0:T(4,128)(2,1)} %param.14) | copy-start | bytes 9437188
  7.2 67.7 %all-reduce.8.cloned.1.call-start = ((), (), s32[]{:S(2)}) async-start(), calls=%async_computation | async-start | bytes 131072
  26.3 24.2 %copy-start.5 = (s32[1,48]{1,0:T(1,128)S(1)}, s32[1,48]{1,0:T(1,128)}, u32[]{:S(2)}) copy-start(s32[1,48]{1,0:T(1,128)} %param.23) | copy-start | bytes 580
  26.3 25.0 %copy-start.4 = (bf16[448]{0:T(512)(128)(2,1)S(1)}, bf16[448]{0:T(512)(128)(2,1)}, u32[]{:S(2)}) copy-start(bf16[448]{0:T(512)(128)(2,1)} %param.18) | copy-start | bytes 2692
  26.3 25.0 %copy-start.7 = (u32[32]{0:T(128)S(1)}, u32[32]{0:T(128)}, u32[]{:S(2)}) copy-start(u32[32]{0:T(128)} %constant.67) | copy-start | bytes 388
  39.6 60.5 %copy-start.2 = (bf16[32,448]{1,0:T(8,128)(2,1)S(1)}, bf16[32,448]{1,0:T(8,128)(2,1)}, u32[]{:S(2)}) copy-start(bf16[32,448]{1,0:T(8,128)(2,1)} %param.15) | copy-start | bytes 86020
  39.6 60.5 %copy-start.3 = (bf16[448]{0:T(512)(128)(2,1)S(1)}, bf16[448]{0:T(512)(128)(2,1)}, u32[]{:S(2)}) copy-start(bf16[448]{0:T(512)(128)(2,1)} %param.16) | copy-start | bytes 2692
  42.1 117.7 %all-reduce.12.cloned.1.call-start = ((), (), s32[]{:S(2)}) async-start(), calls=%async_computation.2 | async-start | bytes 458752 | tf_op jit(solution)/shard_map/psum | solution.py:95
  130.0 4.8 %copy-start.1 = (bf16[3584,32]{0,1:T(8,128)(2,1)S(1)}, bf16[3584,32]{0,1:T(8,128)(2,1)}, u32[]{:S(2)}) copy-start(bf16[3584,32]{0,1:T(8,128)(2,1)} %reshape.80) | copy-start | bytes 688132
  139.5 78.3 %all-reduce.10.cloned.1.call-start = ((), (), s32[]{:S(2)}) async-start(), calls=%async_computation.1 | async-start | bytes 458752
  159.8 4.9 %copy-start.6 = (u32[32]{0:T(128)S(1)}, u32[32]{0:T(128)}, u32[]{:S(2)}) copy-start(u32[32]{0:T(128)} %constant.75) | copy-start | bytes 388
Sparse Core Ops, SparseCore 0:
  42.2 32.5 all-reduce.7
  139.6 20.1 all-reduce.11
  164.7 53.0 all-reduce.9
where the time goes:
time: 226 us
  waiting for transfers between devices  94.3 us (42%)
  blocking collectives  85.6 us (38%)
  matrix products  22.6 us (10%)
  between operations  15.9 us (7%)
  other arithmetic  4.81 us (2%)
  local copies, waits for them, and re-layouts  2.44 us (1%)
    unnamed x5, waiting for transfers between devices  74.1 us
    psum x1, waiting for transfers between devices, shards(): lax.psum(gate_part.astype(jnp.bfloat16), 'heads').astype(jnp.float32)  20.3 us
    all_gather x1, blocking collectives, shards(): queries_all = lax.all_gather(queries, 'blk', axis=0, tiled=True)  15.3 us
    all_gather x1, blocking collectives, shards(): normed_full = lax.all_gather(normed, ('blk', 'rows'), axis=1, tiled=True)  14.2 us
    all_gather x1, blocking collectives, shards(): attn_all = lax.all_gather(attn_own, ('blk', 'rows'), axis=0, tiled=True)  14 us
    psum x1, blocking collectives, shards(): lax.psum(jnp.sum(stream_mid * stream_mid, axis=1), ('blk', 'rows'))  13.6 us
    pmax x1, blocking collectives, shards(): highest = lax.pmax(local_peak, 'blk')  11.8 us
    unnamed x1, blocking collectives  8.38 us
  transfers between devices with their start and end apart: 3, of which 3 were waited for; matrix products, arithmetic and copies ran while one was open for 1% of the time, Pallas kernels for 0%

commit v1 on v0

--- a/solution.py
+++ b/solution.py
@@ -1,6 +1,10 @@
+import functools
+
 import jax
 import jax.numpy as jnp
 from jax import lax
+from jax.experimental import pallas as pl
+from jax.experimental.pallas import tpu as pltpu
 from jax.sharding import PartitionSpec as P
 
 D = 3584
@@ -107,7 +111,531 @@
     return (stream, (down_out * keep_own).astype(jnp.bfloat16))
 
 
+LANES = 128
+MESH = pl.DeviceIdType.MESH
+NEG = -1e30
+
+
+def fits(sizes, queries, src_keys, dec_state, out_weight, gate_weight, down_weight):
+    blocks, heads, rows = sizes
+    tok_dev, local_heads, head_size = queries.shape
+    width = out_weight.shape[1]
+    return (
+        heads == 2
+        and rows == 2
+        and blocks % heads == 0
+        and local_heads == 8
+        and tok_dev == 4
+        and src_keys.shape[1] == 4
+        and src_keys.shape[0] % LANES == 0
+        and head_size == 2 * LANES
+        and width % 64 == 0
+        and gate_weight.shape[0] == width * blocks * rows // heads
+        and gate_weight.shape[1] % (2 * LANES) == 0
+        and down_weight.shape[1] % LANES == 0
+        and dec_state.shape[0] <= 2 * LANES
+        and gate_weight.size * 6 + src_keys.size * 8 <= 40 << 20
+    )
+
+
+def fused(
+    sizes,
+    q_ref,
+    k_hbm,
+    v_hbm,
+    dec_ref,
+    emb_ref,
+    ow_hbm,
+    gain_ref,
+    gate_hbm,
+    up_hbm,
+    down_hbm,
+    len_ref,
+    pos_ref,
+    stream_ref,
+    branch_ref,
+    kbuf,
+    vbuf,
+    sbuf,
+    qall,
+    att_send,
+    att_recv,
+    ag,
+    agf,
+    owbuf,
+    pp_send,
+    pp_recv,
+    xb,
+    sqb,
+    gbuf,
+    ubuf,
+    dbuf,
+    gu,
+    gs_send,
+    gs_recv,
+    acc,
+    dn_send,
+    dn_recv,
+    kv_sem,
+    ow_sem,
+    g_sem,
+    u_sem,
+    d_sem,
+    q_ss,
+    q_rs,
+    a_ss,
+    a_rs,
+    ag_ss,
+    ag_fs,
+    ag_rs,
+    p_ss,
+    p_rs,
+    x_ss,
+    x_fs,
+    x_rs,
+    s_ss,
+    s_rs,
+    gs_ss,
+    gs_rs,
+    dn_ss,
+    dn_rs,
+):
+    nb, nh, nr = sizes
+    nj = nb * nr
+    b = lax.axis_index("blk")
+    h = lax.axis_index("heads")
+    r = lax.axis_index("rows")
+    me = b * nr + r
+    other_row = 1 - r
+    other_head = 1 - h
+    own_rows = q_ref.shape[0]
+    head_size = q_ref.shape[1]
+    kv_heads = k_hbm.shape[1]
+    src_len = k_hbm.shape[0]
+    tokens, width = dec_ref.shape
+    tok_dev = tokens // nj
+    n_heads = own_rows // tok_dev
+    n_chunks = gbuf.shape[0]
+    chunk = gbuf.shape[2]
+    f32 = jnp.float32
+    bf16 = jnp.bfloat16
+
+    for half in range(2):
+        cols = pl.ds(half * LANES, LANES)
+        pltpu.make_async_copy(k_hbm.at[:, :, cols], kbuf.at[half], kv_sem.at[half]).start()
+    for half in range(2):
+        cols = pl.ds(half * LANES, LANES)
+        pltpu.make_async_copy(v_hbm.at[:, :, cols], vbuf.at[half], kv_sem.at[2 + half]).start()
+    pltpu.make_async_copy(ow_hbm, owbuf, ow_sem).start()
+    for c in range(n_chunks):
+        cols = pl.ds(c * chunk, chunk)
+        pltpu.make_async_copy(gate_hbm.at[:, cols], gbuf.at[c], g_sem.at[c]).start()
+        pltpu.make_async_copy(up_hbm.at[:, cols], ubuf.at[c], u_sem.at[c]).start()
+    for c in range(n_chunks):
+        pltpu.make_async_copy(down_hbm.at[pl.ds(c * chunk, chunk)], dbuf.at[c], d_sem.at[c]).start()
+
+    barrier = pltpu.get_barrier_semaphore()
+    for d in range(1, nj):
+        peer = lax.rem(me + d, nj)
+        pl.semaphore_signal(
+            barrier,
+            inc=1,
+            device_id={"blk": peer // nr, "rows": lax.rem(peer, nr)},
+            device_id_type=MESH,
+        )
+    pl.semaphore_signal(barrier, inc=1, device_id={"heads": other_head}, device_id_type=MESH)
+    pl.semaphore_wait(barrier, nj)
+
+    def remote(source, target, send, recv, where):
+        return pltpu.make_async_remote_copy(
+            src_ref=source,
+            dst_ref=target,
+            send_sem=send,
+            recv_sem=recv,
+            device_id=where,
+            device_id_type=MESH,
+        )
+
+    sent = []
+
+    def send(*args):
+        copy = remote(*args)
+        copy.start()
+        sent.append(copy)
+
+    far = [lax.rem(b + d, nb) for d in range(1, nb)]
+    partner = {"rows": other_row}
+
+    for d, pb in enumerate(far):
+        send(q_ref, qall.at[b], q_ss.at[d], q_rs.at[b], {"blk": pb})
+    qall[b] = q_ref[...]
+    for d, pb in enumerate(far):
+        remote(q_ref, qall.at[pb], q_ss.at[d], q_rs.at[pb], {"blk": pb}).wait_recv()
+
+    n_rows = nb * own_rows
+    piece = LANES * kv_heads
+    pieces = src_len // LANES
+    query = qall[...].reshape(n_rows, head_size)
+    row = lax.broadcasted_iota(jnp.int32, (n_rows, piece), 0)
+    col = lax.broadcasted_iota(jnp.int32, (n_rows, piece), 1)
+    fitting = (lax.rem(row, n_heads) // (n_heads // kv_heads)) == lax.rem(col, kv_heads)
+    scale = head_size ** (-0.5)
+    for half in range(2):
+        cols = pl.ds(half * LANES, LANES)
+        pltpu.make_async_copy(k_hbm.at[:, :, cols], kbuf.at[half], kv_sem.at[half]).wait()
+
+    def load(buf, i):
+        parts = [
+            buf[half, pl.ds(i * LANES, LANES)].reshape(piece, LANES) for half in range(2)
+        ]
+        return jnp.concatenate(parts, axis=1)
+
+    def score(i, top):
+        found = lax.dot_general(
+            query, load(kbuf, i), (((1,), (1,)), ((), ())), preferred_element_type=f32
+        )
+        found = jnp.where(fitting, found * scale, NEG)
+        sbuf[i] = found
+        for part in range(kv_heads):
+            top = jnp.maximum(top, found[:, part * LANES : (part + 1) * LANES])
+        return top
+
+    top = lax.fori_loop(0, pieces, score, jnp.full((n_rows, LANES), NEG, f32))
+    peak_bf = jnp.max(top, axis=1, keepdims=True).astype(bf16)
+    left = lax.broadcasted_iota(jnp.int32, (n_rows, LANES), 1) < LANES // 2
+    peak = peak_bf.astype(f32)
+    for half in range(2):
+        cols = pl.ds(half * LANES, LANES)
+        pltpu.make_async_copy(v_hbm.at[:, :, cols], vbuf.at[half], kv_sem.at[2 + half]).wait()
+
+    def weigh(i, carry):
+        total, summed = carry
+        weight = jnp.exp(sbuf[i] - peak)
+        for part in range(kv_heads):
+            total = total + weight[:, part * LANES : (part + 1) * LANES]
+        summed = summed + jnp.dot(weight.astype(bf16), load(vbuf, i), preferred_element_type=f32)
+        return total, summed
+
+    total, summed = lax.fori_loop(
+        0, pieces, weigh, (jnp.zeros((n_rows, LANES), f32), jnp.zeros((n_rows, head_size), f32))
+    )
+    total = jnp.sum(total, axis=1, keepdims=True)
+    att_send[:, :, :head_size] = (summed / total).astype(bf16).reshape(nb, own_rows, head_size)
+    stats = jnp.where(left, peak, total).astype(bf16)
+    att_send[:, :, head_size:] = stats.reshape(nb, own_rows, LANES)
+
+    for d, pb in enumerate(far):
+        send(att_send.at[pb], att_recv.at[b], a_ss.at[d], a_rs.at[b], {"blk": pb})
+    att_recv[b] = att_send[b]
+    for d, pb in enumerate(far):
+        remote(
+            att_send.at[pb], att_recv.at[pb], a_ss.at[d], a_rs.at[pb], {"blk": pb}
+        ).wait_recv()
+    got = [att_recv[i].astype(f32) for i in range(nb)]
+    peaks = [x[:, head_size : head_size + 1] for x in got]
+    totals = [x[:, head_size + LANES // 2 : head_size + LANES // 2 + 1] for x in got]
+    highest = peaks[0]
+    for x in peaks[1:]:
+        highest = jnp.maximum(highest, x)
+    shares = [t * jnp.exp(p - highest) for t, p in zip(totals, peaks)]
+    numer = shares[0] * got[0][:, :head_size]
+    denom = shares[0]
+    for x, share in zip(got[1:], shares[1:]):
+        numer = numer + share * x[:, :head_size]
+        denom = denom + share
+    ag[me] = (numer / denom).astype(bf16)
+
+    for d, pb in enumerate(far):
+        send(ag.at[me], ag.at[me], ag_ss.at[d], ag_rs.at[me], {"blk": pb})
+    send(ag.at[me], ag.at[me], ag_fs.at[b], ag_rs.at[me], partner)
+    for d, pb in enumerate(far):
+        j = pb * nr + r
+        remote(ag.at[me], ag.at[j], ag_ss.at[d], ag_rs.at[j], {"blk": pb}).wait_recv()
+        send(ag.at[j], ag.at[j], ag_fs.at[pb], ag_rs.at[j], partner)
+    for pb in [b] + far:
+        j = pb * nr + other_row
+        remote(ag.at[j], ag.at[j], ag_fs.at[pb], ag_rs.at[j], partner).wait_recv()
+    everyone = ag[...].astype(f32).reshape(nj * own_rows, head_size)
+    for half in range(2):
+        agf[half] = everyone[:, half * LANES : (half + 1) * LANES]
+    pltpu.make_async_copy(ow_hbm, owbuf, ow_sem).wait()
+    product = jnp.zeros((tokens, width), f32)
+    for n in range(n_heads):
+        parts = [agf[half, pl.ds(n, tokens, stride=n_heads), :] for half in range(2)]
+        one = jnp.concatenate(parts, axis=1).astype(bf16)
+        product = product + jnp.dot(
+            one, owbuf[n * head_size : (n + 1) * head_size, :], preferred_element_type=f32
+        )
+    pp_send[...] = product.astype(bf16)
+    send(pp_send, pp_recv, p_ss, p_rs, {"heads": other_head})
+
+    def masks(start, count):
+        token = lax.broadcasted_iota(jnp.int32, (count, 1), 0) + start
+        place = lax.rem(token, LEN)
+        which = token // LEN
+        valid = jnp.zeros((count, 1), f32)
+        hidden_slot = jnp.zeros((count, 1), f32)
+        for c in range(pos_ref.shape[0]):
+            here = (which == c).astype(f32)
+            valid = valid + here * (place < len_ref[c]).astype(f32)
+            same = (pos_ref[c : c + 1, :] == place).astype(f32)
+            hidden_slot = hidden_slot + here * jnp.max(same, axis=1, keepdims=True)
+        return valid, hidden_slot
+
+    valid, hidden_slot = masks(0, tokens)
+    base = jnp.where(hidden_slot > 0.5, emb_ref[...].astype(f32), dec_ref[...].astype(f32))
+    gain = gain_ref[...].astype(f32)
+    remote(pp_send, pp_recv, p_ss, p_rs, {"heads": other_head}).wait_recv()
+    mid = base + (pp_send[...].astype(f32) + pp_recv[...].astype(f32))
+    xb[me] = (mid * gain).astype(bf16)
+
+    per = nb // nh
+    mine = (b // per) == h
+
+    @pl.when(mine)
+    def _():
+        for d, pb in enumerate(far):
+            remote(xb.at[me], xb.at[me], x_ss.at[d], x_rs.at[me], {"blk": pb}).start()
+        remote(xb.at[me], xb.at[me], x_fs.at[lax.rem(b, per)], x_rs.at[me], partner).start()
+
+    sqb[me] = jnp.broadcast_to(jnp.sum(mid * mid, axis=1, keepdims=True), (tokens, LANES))
+    stream_ref[...] = (mid * valid).astype(bf16)
+    for d in range(1, nj):
+        peer = lax.rem(me + d, nj)
+        send(
+            sqb.at[me],
+            sqb.at[me],
+            s_ss.at[d],
+            s_rs.at[me],
+            {"blk": peer // nr, "rows": lax.rem(peer, nr)},
+        )
+    for k in range(per):
+        sb = h * per + k
+        j = sb * nr + r
+
+        @pl.when(sb != b)
+        def _():
+            remote(xb.at[j], xb.at[j], x_ss.at[0], x_rs.at[j], {"blk": sb}).wait_recv()
+            remote(xb.at[j], xb.at[j], x_fs.at[k], x_rs.at[j], partner).start()
+
+    for k in range(per):
+        j = (h * per + k) * nr + other_row
+        remote(xb.at[j], xb.at[j], x_fs.at[k], x_rs.at[j], partner).wait_recv()
+    features = jnp.concatenate([xb[h * per * nr + k] for k in range(per * nr)], axis=1)
+
+    def project(c, carry):
+        cols = pl.ds(pl.multiple_of(c * chunk, chunk), chunk)
+        pltpu.make_async_copy(gate_hbm.at[:, cols], gbuf.at[c], g_sem.at[c]).wait()
+        gate = jnp.dot(features, gbuf[c], preferred_element_type=f32)
+        gu[c, 0] = gate
+        gs_send[c, 0] = gate.astype(bf16)
+        pltpu.make_async_copy(up_hbm.at[:, cols], ubuf.at[c], u_sem.at[c]).wait()
+        up = jnp.dot(features, ubuf[c], preferred_element_type=f32)
+        gu[c, 1] = up
+        gs_send[c, 1] = up.astype(bf16)
+        remote(
+            gs_send.at[c], gs_recv.at[c], gs_ss.at[c], gs_rs.at[c], {"heads": other_head}
+        ).start()
+        return carry
+
+    lax.fori_loop(0, n_chunks, project, 0)
+
+    squares = sqb[me]
+    for d in range(1, nj):
+        peer = lax.rem(me + d, nj)
+        remote(
+            sqb.at[peer],
+            sqb.at[peer],
+            s_ss.at[d],
+            s_rs.at[peer],
+            {"blk": peer // nr, "rows": lax.rem(peer, nr)},
+        ).wait_recv()
+        squares = squares + sqb[peer]
+    inverse = lax.rsqrt(squares[:, :1] / (width * nj) + 1e-06)
+
+    acc[...] = jnp.zeros_like(acc)
+
+    def contract(c, carry):
+        remote(
+            gs_send.at[c], gs_recv.at[c], gs_ss.at[c], gs_rs.at[c], {"heads": other_head}
+        ).wait()
+        gate = (gu[c, 0] + gs_recv[c, 0].astype(f32)) * inverse
+        up = (gu[c, 1] + gs_recv[c, 1].astype(f32)) * inverse
+        hidden = (jax.nn.gelu(gate, approximate=True) * up).astype(bf16)
+        pltpu.make_async_copy(
+            down_hbm.at[pl.ds(pl.multiple_of(c * chunk, chunk), chunk)], dbuf.at[c], d_sem.at[c]
+        ).wait()
+        acc[...] += jnp.dot(hidden, dbuf[c], preferred_element_type=f32)
+        return carry
+
+    lax.fori_loop(0, n_chunks, contract, 0)
+
+    for j in range(nj):
+        dn_send[j] = acc[j * tok_dev : (j + 1) * tok_dev, :].astype(bf16)
+    for d in range(1, nj):
+        peer = lax.rem(me + d, nj)
+        send(
+            dn_send.at[peer],
+            dn_recv.at[me],
+            dn_ss.at[d],
+            dn_rs.at[me],
+            {"blk": peer // nr, "rows": lax.rem(peer, nr)},
+        )
+    result = dn_send[me].astype(f32)
+    for d in range(1, nj):
+        peer = lax.rem(me + d, nj)
+        remote(
+            dn_send.at[peer],
+            dn_recv.at[peer],
+            dn_ss.at[d],
+            dn_rs.at[peer],
+            {"blk": peer // nr, "rows": lax.rem(peer, nr)},
+        ).wait_recv()
+        result = result + dn_recv[peer].astype(f32)
+    branch_ref[...] = (result * masks(me * tok_dev, tok_dev)[0]).astype(bf16)
+
+    for copy in sent:
+        copy.wait_send()
+
+    @pl.when(mine)
+    def _():
+        for d, pb in enumerate(far):
+            remote(xb.at[me], xb.at[me], x_ss.at[d], x_rs.at[me], {"blk": pb}).wait_send()
+
+    for k in range(per):
+        remote(xb.at[me], xb.at[me], x_fs.at[k], x_rs.at[me], partner).wait_send()
+
+
+def kernel_call(sizes, *args):
+    (
+        queries,
+        src_keys,
+        src_values,
+        dec_state,
+        mask_embed,
+        out_weight,
+        norm_gain,
+        gate_weight,
+        up_weight,
+        down_weight,
+        cand_lengths,
+        masked_pos,
+    ) = args
+    nb, nh, nr = sizes
+    nj = nb * nr
+    tok_dev, local_heads, head_size = queries.shape
+    own_rows = tok_dev * local_heads
+    src_len, kv_heads, _ = src_keys.shape
+    tokens, width = dec_state.shape
+    depth, hidden = gate_weight.shape
+    out_width = down_weight.shape[1]
+    chunk = 2 * LANES
+    n_chunks = hidden // chunk
+    f32 = jnp.float32
+    bf16 = jnp.bfloat16
+    dma = pltpu.SemaphoreType.DMA
+    vmem = pl.BlockSpec(memory_space=pltpu.VMEM)
+    anywhere = pl.BlockSpec(memory_space=pl.ANY)
+    smem = pl.BlockSpec(memory_space=pltpu.SMEM)
+    scratch = [
+        pltpu.VMEM((2, src_len, kv_heads, LANES), bf16),
+        pltpu.VMEM((2, src_len, kv_heads, LANES), bf16),
+        pltpu.VMEM((src_len // LANES, nb * own_rows, kv_heads * LANES), f32),
+        pltpu.VMEM((nb, own_rows, head_size), bf16),
+        pltpu.VMEM((nb, own_rows, head_size + LANES), bf16),
+        pltpu.VMEM((nb, own_rows, head_size + LANES), bf16),
+        pltpu.VMEM((nj, own_rows, head_size), bf16),
+        pltpu.VMEM((2, nj * own_rows, LANES), f32),
+        pltpu.VMEM(out_weight.shape, bf16),
+        pltpu.VMEM((tokens, width), bf16),
+        pltpu.VMEM((tokens, width), bf16),
+        pltpu.VMEM((nj, tokens, width), bf16),
+        pltpu.VMEM((nj, tokens, LANES), f32),
+        pltpu.VMEM((n_chunks, depth, chunk), bf16),
+        pltpu.VMEM((n_chunks, depth, chunk), bf16),
+        pltpu.VMEM((n_chunks, chunk, out_width), bf16),
+        pltpu.VMEM((n_chunks, 2, tokens, chunk), f32),
+        pltpu.VMEM((n_chunks, 2, tokens, chunk), bf16),
+        pltpu.VMEM((n_chunks, 2, tokens, chunk), bf16),
+        pltpu.VMEM((tokens, out_width), f32),
+        pltpu.VMEM((nj, tok_dev, out_width), bf16),
+        pltpu.VMEM((nj, tok_dev, out_width), bf16),
+        dma((4,)),
+        dma,
+        dma((n_chunks,)),
+        dma((n_chunks,)),
+        dma((n_chunks,)),
+        dma((nb,)),
+        dma((nb,)),
+        dma((nb,)),
+        dma((nb,)),
+        dma((nb,)),
+        dma((nb,)),
+        dma((nj,)),
+        dma,
+        dma,
+        dma((nb,)),
+        dma((nb,)),
+        dma((nj,)),
+        dma((nj,)),
+        dma((nj,)),
+        dma((n_chunks,)),
+        dma((n_chunks,)),
+        dma((nj,)),
+        dma((nj,)),
+    ]
+    return tuple(
+        pl.pallas_call(
+            functools.partial(fused, sizes),
+            out_shape=(
+                jax.ShapeDtypeStruct((tokens, width), bf16),
+                jax.ShapeDtypeStruct((tok_dev, out_width), bf16),
+            ),
+            in_specs=[
+                vmem,
+                anywhere,
+                anywhere,
+                vmem,
+                vmem,
+                anywhere,
+                vmem,
+                anywhere,
+                anywhere,
+                anywhere,
+                smem,
+                vmem,
+            ],
+            out_specs=(vmem, vmem),
+            scratch_shapes=scratch,
+            compiler_params=pltpu.CompilerParams(
+                collective_id=0, has_side_effects=True, vmem_limit_bytes=56 << 20
+            ),
+        )(
+            queries.reshape(own_rows, head_size),
+            src_keys,
+            src_values,
+            dec_state,
+            mask_embed.reshape(1, width),
+            out_weight,
+            norm_gain.reshape(1, width),
+            gate_weight,
+            up_weight,
+            down_weight,
+            cand_lengths,
+            masked_pos,
+        )
+    )
+
+
+def step(sizes, *args):
+    queries, src_keys, _, dec_state, _, out_weight, _, gate_weight, _, down_weight, _, _ = args
+    if fits(sizes, queries, src_keys, dec_state, out_weight, gate_weight, down_weight):
+        return kernel_call(sizes, *args)
+    return shards(*args)
+
+
 def solution(mesh):
+    sizes = tuple(mesh.shape[name] for name in ("blk", "heads", "rows"))
     placed = (
         P(("groups", "blk", "rows"), "heads", None),
         P(("groups", "blk"), "heads", None),
@@ -123,7 +651,7 @@
         P("groups", None),
     )
     return jax.shard_map(
-        shards,
+        functools.partial(step, sizes),
         mesh=mesh,
         in_specs=placed,
         out_specs=(P("groups", ("blk", "rows")), P(("groups", "blk", "rows"), "heads")),

time: 226 us -> 56.7 us (0.25)
  waiting for transfers between devices: 94.3 us -> 0 us
  blocking collectives: 85.6 us -> 0 us
  Pallas kernels: 0 us -> 46 us
  matrix products: 22.6 us -> 0 us
  between operations: 15.9 us -> 1.29 us
  local copies, waits for them, and re-layouts: 2.44 us -> 9.03 us
  other arithmetic: 4.81 us -> 0 us
    unnamed x5 -> x0, waiting for transfers between devices: 74.1 us -> none
    pallas_call x0 -> x1, Pallas kernels: none -> 46 us  [kernel_call(): pl.pallas_call(functools.partial(fused, sizes), out_shape=(jax.ShapeDtype...]
    all_gather x3 -> x0, blocking collectives: 43.5 us -> none  [the longest x1 15.3 us: shards(): queries_all = lax.all_gather(queries, 'blk', axis=0, tiled=True)]
    dot_general x6 -> x0, matrix products: 22.6 us -> none  [the longest x1 4.81 us: shards(): jnp.dot(column_block, up_weight, preferred_element_type=jnp.float32)]
    psum x2 -> x0, blocking collectives: 22 us -> none  [the longest x1 13.6 us: shards(): lax.psum(jnp.sum(stream_mid * stream_mid, axis=1), ('blk', 'rows'))]
    psum x1 -> x0, waiting for transfers between devices: 20.3 us -> none  [shards(): lax.psum(gate_part.astype(jnp.bfloat16), 'heads').astype(jnp.float32)]
    pmax x1 -> x0, blocking collectives: 11.8 us -> none  [shards(): highest = lax.pmax(local_peak, 'blk')]
    unnamed x1 -> x0, blocking collectives: 8.38 us -> none
  transfers between devices with their start and end apart: 3 -> 0, of which waited for: 3 -> 0; matrix products, arithmetic and copies ran while one was open for 1% -> 0% of each run, Pallas kernels for 0% -> 0%
where the time goes in v1:
time: 56.7 us; the launch traced here: 56.3 us
  Pallas kernels  46 us (81%)
  local copies, waits for them, and re-layouts  9.03 us (16%)
  between operations  1.29 us (2%)
    pallas_call x1, Pallas kernels, kernel_call(): pl.pallas_call(functools.partial(fused, sizes), out_shape=(jax.ShapeDtype...  46 us
    unnamed x3, local copies, waits for them, and re-layouts  6.51 us
    reshape x1, local copies, waits for them, and re-layouts, kernel_call(): mask_embed.reshape(1, width)  1.26 us
    reshape x1, local copies, waits for them, and re-layouts, kernel_call(): norm_gain.reshape(1, width)  1.26 us

profile of v1, /device:TPU:0, one launch (start us, length us, event | category | flops | bytes accessed | tf_op | source)
XLA Modules:
  0.0 56.3 jit_solution(12005694317334432179)
XLA Ops:
  1.3 1.3 %reshape.14.emb_ref = bf16[1,448]{1,0:T(2,128)(2,1)} reshape(bf16[448]{0:T(512)(128)(2,1)} %param.16) | data formatting | bytes 1792 | tf_op jit(solution)/shard_map/reshape | solution.py:618
  2.5 1.3 %reshape.15.gain_ref = bf16[1,448]{1,0:T(2,128)(2,1)} reshape(bf16[448]{0:T(512)(128)(2,1)} %param.18) | data formatting | bytes 1792 | tf_op jit(solution)/shard_map/reshape | solution.py:620
  3.8 3.8 %copy.14.ow_hbm = bf16[2048,448]{1,0:T(8,128)(2,1)} copy(bf16[2048,448]{0,1:T(8,128)(2,1)} %param.17) | data formatting | bytes 3670016 | tf_op args[5]
  7.6 46.0 %shard_map.131 = (bf16[32,448]{1,0:T(8,128)(2,1)}, bf16[4,1792]{1,0:T(4,128)(2,1)}) custom-call(bf16[32,256]{1,0:T(8,128)(2,1)} %bitcast.1, bf16[1536,4,256]{2,1,0:T(4,128)(2,1)} %k_hbm.1, bf16[1536,4,256]{2,1,0:T(4,128)(2,1)} %v_hbm.1, bf16[32,448]{1,0:T(8,128)(2,1)} %dec_ref.1, bf16[1,448]{1,0:T(2,128)(2,1)} %reshape.14.emb_ref, ...), custom_call_target="tpu_custom_call" | custom-call | tf_op jit(solution)/shard_map/pallas_call | solution.py:588
  53.6 1.4 %copy.18 = bf16[32,448]{1,0:T(8,128)(2,1)} copy(bf16[32,448]{1,0:T(8,128)(2,1)} %get-tuple-element.4) | data formatting | bytes 57344
  55.0 1.3 %copy.19 = bf16[4,1792]{1,0:T(4,128)(2,1)} copy(bf16[4,1792]{1,0:T(4,128)(2,1)} %get-tuple-element.5) | data formatting | bytes 28672

commit v2 on v1

--- a/solution.py
+++ b/solution.py
@@ -132,7 +132,7 @@
         and width % 64 == 0
         and gate_weight.shape[0] == width * blocks * rows // heads
         and gate_weight.shape[1] % (2 * LANES) == 0
-        and down_weight.shape[1] % LANES == 0
+        and down_weight.shape[1] % (2 * LANES) == 0
         and dec_state.shape[0] <= 2 * LANES
         and gate_weight.size * 6 + src_keys.size * 8 <= 40 << 20
     )
@@ -143,15 +143,15 @@
     q_ref,
     k_hbm,
     v_hbm,
-    dec_ref,
-    emb_ref,
+    dec_hbm,
+    emb_hbm,
     ow_hbm,
-    gain_ref,
+    gain_hbm,
     gate_hbm,
     up_hbm,
     down_hbm,
-    len_ref,
-    pos_ref,
+    len_hbm,
+    pos_hbm,
     stream_ref,
     branch_ref,
     kbuf,
@@ -173,9 +173,16 @@
     gu,
     gs_send,
     gs_recv,
+    units,
     acc,
     dn_send,
     dn_recv,
+    dec_ref,
+    emb_ref,
+    gain_ref,
+    len_ref,
+    pos_ref,
+    small_sem,
     kv_sem,
     ow_sem,
     g_sem,
@@ -212,7 +219,7 @@
     head_size = q_ref.shape[1]
     kv_heads = k_hbm.shape[1]
     src_len = k_hbm.shape[0]
-    tokens, width = dec_ref.shape
+    tokens, width = dec_hbm.shape
     tok_dev = tokens // nj
     n_heads = own_rows // tok_dev
     n_chunks = gbuf.shape[0]
@@ -220,20 +227,27 @@
     f32 = jnp.float32
     bf16 = jnp.bfloat16
 
+    small = [
+        pltpu.make_async_copy(source, target, small_sem.at[i])
+        for i, (source, target) in enumerate(
+            [
+                (q_ref, qall.at[b]),
+                (dec_hbm, dec_ref),
+                (emb_hbm, emb_ref),
+                (gain_hbm, gain_ref),
+                (len_hbm, len_ref),
+                (pos_hbm, pos_ref),
+            ]
+        )
+    ]
+    for copy in small:
+        copy.start()
     for half in range(2):
         cols = pl.ds(half * LANES, LANES)
         pltpu.make_async_copy(k_hbm.at[:, :, cols], kbuf.at[half], kv_sem.at[half]).start()
     for half in range(2):
         cols = pl.ds(half * LANES, LANES)
         pltpu.make_async_copy(v_hbm.at[:, :, cols], vbuf.at[half], kv_sem.at[2 + half]).start()
-    pltpu.make_async_copy(ow_hbm, owbuf, ow_sem).start()
-    for c in range(n_chunks):
-        cols = pl.ds(c * chunk, chunk)
-        pltpu.make_async_copy(gate_hbm.at[:, cols], gbuf.at[c], g_sem.at[c]).start()
-        pltpu.make_async_copy(up_hbm.at[:, cols], ubuf.at[c], u_sem.at[c]).start()
-    for c in range(n_chunks):
-        pltpu.make_async_copy(down_hbm.at[pl.ds(c * chunk, chunk)], dbuf.at[c], d_sem.at[c]).start()
-
     barrier = pltpu.get_barrier_semaphore()
     for d in range(1, nj):
         peer = lax.rem(me + d, nj)
@@ -268,13 +282,35 @@
 
     for d, pb in enumerate(far):
         send(q_ref, qall.at[b], q_ss.at[d], q_rs.at[b], {"blk": pb})
-    qall[b] = q_ref[...]
+    small[0].wait()
+
+    for copy in small[1:]:
+        copy.wait()
+
+    def masks(start, count):
+        token = lax.broadcasted_iota(jnp.int32, (count, 1), 0) + start
+        place = lax.rem(token, LEN)
+        which = token // LEN
+        valid = jnp.zeros((count, 1), f32)
+        hidden_slot = jnp.zeros((count, 1), f32)
+        for c in range(pos_ref.shape[0]):
+            here = (which == c).astype(f32)
+            valid = valid + here * (place < len_ref[c]).astype(f32)
+            same = (pos_ref[c : c + 1, :] == place).astype(f32)
+            hidden_slot = hidden_slot + here * jnp.max(same, axis=1, keepdims=True)
+        return valid, hidden_slot
+
+    valid, hidden_slot = masks(0, tokens)
+    own_valid = masks(me * tok_dev, tok_dev)[0]
+    base = jnp.where(hidden_slot > 0.5, emb_ref[...].astype(f32)[None, :], dec_ref[...].astype(f32))
+    gain = gain_ref[...].astype(f32)[None, :]
     for d, pb in enumerate(far):
         remote(q_ref, qall.at[pb], q_ss.at[d], q_rs.at[pb], {"blk": pb}).wait_recv()
 
     n_rows = nb * own_rows
     piece = LANES * kv_heads
     pieces = src_len // LANES
+    unroll = 4 if pieces % 4 == 0 else 1
     query = qall[...].reshape(n_rows, head_size)
     row = lax.broadcasted_iota(jnp.int32, (n_rows, piece), 0)
     col = lax.broadcasted_iota(jnp.int32, (n_rows, piece), 1)
@@ -300,13 +336,30 @@
             top = jnp.maximum(top, found[:, part * LANES : (part + 1) * LANES])
         return top
 
-    top = lax.fori_loop(0, pieces, score, jnp.full((n_rows, LANES), NEG, f32))
+    def several(one):
+        def run(i, carry):
+            for u in range(unroll):
+                carry = one(i * unroll + u, carry)
+            return carry
+
+        return run
+
+    top = lax.fori_loop(
+        0, pieces // unroll, several(score), jnp.full((n_rows, LANES), NEG, f32)
+    )
     peak_bf = jnp.max(top, axis=1, keepdims=True).astype(bf16)
     left = lax.broadcasted_iota(jnp.int32, (n_rows, LANES), 1) < LANES // 2
     peak = peak_bf.astype(f32)
     for half in range(2):
         cols = pl.ds(half * LANES, LANES)
         pltpu.make_async_copy(v_hbm.at[:, :, cols], vbuf.at[half], kv_sem.at[2 + half]).wait()
+    pltpu.make_async_copy(ow_hbm, owbuf, ow_sem).start()
+    for c in range(n_chunks):
+        cols = pl.ds(c * chunk, chunk)
+        pltpu.make_async_copy(gate_hbm.at[:, cols], gbuf.at[c], g_sem.at[c]).start()
+        pltpu.make_async_copy(up_hbm.at[:, cols], ubuf.at[c], u_sem.at[c]).start()
+    for c in range(n_chunks):
+        pltpu.make_async_copy(down_hbm.at[pl.ds(c * chunk, chunk)], dbuf.at[c], d_sem.at[c]).start()
 
     def weigh(i, carry):
         total, summed = carry
@@ -317,7 +370,10 @@
         return total, summed
 
     total, summed = lax.fori_loop(
-        0, pieces, weigh, (jnp.zeros((n_rows, LANES), f32), jnp.zeros((n_rows, head_size), f32))
+        0,
+        pieces // unroll,
+        several(weigh),
+        (jnp.zeros((n_rows, LANES), f32), jnp.zeros((n_rows, head_size), f32)),
     )
     total = jnp.sum(total, axis=1, keepdims=True)
     att_send[:, :, :head_size] = (summed / total).astype(bf16).reshape(nb, own_rows, head_size)
@@ -363,28 +419,15 @@
     for n in range(n_heads):
         parts = [agf[half, pl.ds(n, tokens, stride=n_heads), :] for half in range(2)]
         one = jnp.concatenate(parts, axis=1).astype(bf16)
-        product = product + jnp.dot(
-            one, owbuf[n * head_size : (n + 1) * head_size, :], preferred_element_type=f32
+        product = product + lax.dot_general(
+            one,
+            owbuf[:, n * head_size : (n + 1) * head_size],
+            (((1,), (1,)), ((), ())),
+            preferred_element_type=f32,
         )
     pp_send[...] = product.astype(bf16)
     send(pp_send, pp_recv, p_ss, p_rs, {"heads": other_head})
 
-    def masks(start, count):
-        token = lax.broadcasted_iota(jnp.int32, (count, 1), 0) + start
-        place = lax.rem(token, LEN)
-        which = token // LEN
-        valid = jnp.zeros((count, 1), f32)
-        hidden_slot = jnp.zeros((count, 1), f32)
-        for c in range(pos_ref.shape[0]):
-            here = (which == c).astype(f32)
-            valid = valid + here * (place < len_ref[c]).astype(f32)
-            same = (pos_ref[c : c + 1, :] == place).astype(f32)
-            hidden_slot = hidden_slot + here * jnp.max(same, axis=1, keepdims=True)
-        return valid, hidden_slot
-
-    valid, hidden_slot = masks(0, tokens)
-    base = jnp.where(hidden_slot > 0.5, emb_ref[...].astype(f32), dec_ref[...].astype(f32))
-    gain = gain_ref[...].astype(f32)
     remote(pp_send, pp_recv, p_ss, p_rs, {"heads": other_head}).wait_recv()
     mid = base + (pp_send[...].astype(f32) + pp_recv[...].astype(f32))
     xb[me] = (mid * gain).astype(bf16)
@@ -453,6 +496,7 @@
         squares = squares + sqb[peer]
     inverse = lax.rsqrt(squares[:, :1] / (width * nj) + 1e-06)
 
+    span = acc.shape[2]
     acc[...] = jnp.zeros_like(acc)
 
     def contract(c, carry):
@@ -462,37 +506,53 @@
         gate = (gu[c, 0] + gs_recv[c, 0].astype(f32)) * inverse
         up = (gu[c, 1] + gs_recv[c, 1].astype(f32)) * inverse
         hidden = (jax.nn.gelu(gate, approximate=True) * up).astype(bf16)
+        units[c] = hidden
         pltpu.make_async_copy(
             down_hbm.at[pl.ds(pl.multiple_of(c * chunk, chunk), chunk)], dbuf.at[c], d_sem.at[c]
         ).wait()
-        acc[...] += jnp.dot(hidden, dbuf[c], preferred_element_type=f32)
+        acc[0] += jnp.dot(hidden, dbuf[c, :, :span], preferred_element_type=f32)
         return carry
 
     lax.fori_loop(0, n_chunks, contract, 0)
 
-    for j in range(nj):
-        dn_send[j] = acc[j * tok_dev : (j + 1) * tok_dev, :].astype(bf16)
-    for d in range(1, nj):
+    def peer_of(d):
         peer = lax.rem(me + d, nj)
-        send(
-            dn_send.at[peer],
-            dn_recv.at[me],
-            dn_ss.at[d],
-            dn_rs.at[me],
-            {"blk": peer // nr, "rows": lax.rem(peer, nr)},
-        )
-    result = dn_send[me].astype(f32)
-    for d in range(1, nj):
-        peer = lax.rem(me + d, nj)
-        remote(
-            dn_send.at[peer],
-            dn_recv.at[peer],
-            dn_ss.at[d],
-            dn_rs.at[peer],
-            {"blk": peer // nr, "rows": lax.rem(peer, nr)},
-        ).wait_recv()
-        result = result + dn_recv[peer].astype(f32)
-    branch_ref[...] = (result * masks(me * tok_dev, tok_dev)[0]).astype(bf16)
+        return peer, {"blk": peer // nr, "rows": lax.rem(peer, nr)}
+
+    def hand_out(part):
+        for j in range(nj):
+            dn_send[part, j] = acc[part, j * tok_dev : (j + 1) * tok_dev, :].astype(bf16)
+        for d in range(1, nj):
+            peer, where = peer_of(d)
+            send(
+                dn_send.at[part, peer],
+                dn_recv.at[part, me],
+                dn_ss.at[part, d],
+                dn_rs.at[part, me],
+                where,
+            )
+
+    hand_out(0)
+
+    def contract_rest(c, carry):
+        acc[1] += jnp.dot(units[c], dbuf[c, :, span:], preferred_element_type=f32)
+        return carry
+
+    lax.fori_loop(0, n_chunks, contract_rest, 0)
+    hand_out(1)
+    for part in range(2):
+        result = dn_send[part, me].astype(f32)
+        for d in range(1, nj):
+            peer, where = peer_of(d)
+            remote(
+                dn_send.at[part, peer],
+                dn_recv.at[part, peer],
+                dn_ss.at[part, d],
+                dn_rs.at[part, peer],
+                where,
+            ).wait_recv()
+            result = result + dn_recv[part, peer].astype(f32)
+        branch_ref[:, part * span : (part + 1) * span] = (result * own_valid).astype(bf16)
 
     for copy in sent:
         copy.wait_send()
@@ -536,7 +596,6 @@
     dma = pltpu.SemaphoreType.DMA
     vmem = pl.BlockSpec(memory_space=pltpu.VMEM)
     anywhere = pl.BlockSpec(memory_space=pl.ANY)
-    smem = pl.BlockSpec(memory_space=pltpu.SMEM)
     scratch = [
         pltpu.VMEM((2, src_len, kv_heads, LANES), bf16),
         pltpu.VMEM((2, src_len, kv_heads, LANES), bf16),
@@ -546,7 +605,7 @@
         pltpu.VMEM((nb, own_rows, head_size + LANES), bf16),
         pltpu.VMEM((nj, own_rows, head_size), bf16),
         pltpu.VMEM((2, nj * own_rows, LANES), f32),
-        pltpu.VMEM(out_weight.shape, bf16),
+        pltpu.VMEM(out_weight.shape[::-1], bf16),
         pltpu.VMEM((tokens, width), bf16),
         pltpu.VMEM((tokens, width), bf16),
         pltpu.VMEM((nj, tokens, width), bf16),
@@ -557,9 +616,16 @@
         pltpu.VMEM((n_chunks, 2, tokens, chunk), f32),
         pltpu.VMEM((n_chunks, 2, tokens, chunk), bf16),
         pltpu.VMEM((n_chunks, 2, tokens, chunk), bf16),
-        pltpu.VMEM((tokens, out_width), f32),
-        pltpu.VMEM((nj, tok_dev, out_width), bf16),
-        pltpu.VMEM((nj, tok_dev, out_width), bf16),
+        pltpu.VMEM((n_chunks, tokens, chunk), bf16),
+        pltpu.VMEM((2, tokens, out_width // 2), f32),
+        pltpu.VMEM((2, nj, tok_dev, out_width // 2), bf16),
+        pltpu.VMEM((2, nj, tok_dev, out_width // 2), bf16),
+        pltpu.VMEM(dec_state.shape, bf16),
+        pltpu.VMEM(mask_embed.shape, bf16),
+        pltpu.VMEM(norm_gain.shape, bf16),
+        pltpu.SMEM(cand_lengths.shape, jnp.int32),
+        pltpu.VMEM(masked_pos.shape, jnp.int32),
+        dma((6,)),
         dma((4,)),
         dma,
         dma((n_chunks,)),
@@ -581,30 +647,17 @@
         dma((nj,)),
         dma((n_chunks,)),
         dma((n_chunks,)),
-        dma((nj,)),
-        dma((nj,)),
+        dma((2, nj)),
+        dma((2, nj)),
     ]
-    return tuple(
+    results = tuple(
         pl.pallas_call(
             functools.partial(fused, sizes),
             out_shape=(
                 jax.ShapeDtypeStruct((tokens, width), bf16),
                 jax.ShapeDtypeStruct((tok_dev, out_width), bf16),
             ),
-            in_specs=[
-                vmem,
-                anywhere,
-                anywhere,
-                vmem,
-                vmem,
-                anywhere,
-                vmem,
-                anywhere,
-                anywhere,
-                anywhere,
-                smem,
-                vmem,
-            ],
+            in_specs=[anywhere] * 12,
             out_specs=(vmem, vmem),
             scratch_shapes=scratch,
             compiler_params=pltpu.CompilerParams(
@@ -615,9 +668,9 @@
             src_keys,
             src_values,
             dec_state,
-            mask_embed.reshape(1, width),
-            out_weight,
-            norm_gain.reshape(1, width),
+            mask_embed,
+            out_weight.T,
+            norm_gain,
             gate_weight,
             up_weight,
             down_weight,
@@ -625,6 +678,19 @@
             masked_pos,
         )
     )
+    return tuple(
+        pl.pallas_call(
+            hand_on,
+            out_shape=tuple(jax.ShapeDtypeStruct(x.shape, x.dtype) for x in results),
+            in_specs=[vmem, vmem],
+            out_specs=(vmem, vmem),
+        )(*results)
+    )
+
+
+def hand_on(stream_in, branch_in, stream_out, branch_out):
+    stream_out[...] = stream_in[...]
+    branch_out[...] = branch_in[...]
 
 
 def step(sizes, *args):

time: 56.7 us -> 46.7 us (0.82)
  local copies, waits for them, and re-layouts: 9.03 us -> 0 us
  Pallas kernels: 46 us -> 45.2 us
    unnamed x3 -> x0, local copies, waits for them, and re-layouts: 6.51 us -> none
    reshape x2 -> x0, local copies, waits for them, and re-layouts: 2.52 us -> none  [the longest x1 1.26 us: kernel_call(): mask_embed.reshape(1, width)]
    pallas_call x1, Pallas kernels: 46 us -> 43.8 us  [kernel_call(): pl.pallas_call(functools.partial(fused, sizes), out_shape=(jax.ShapeDtype...]
    pallas_call x0 -> x1, Pallas kernels: none -> 1.38 us  [kernel_call(): pl.pallas_call(hand_on, out_shape=tuple((jax.ShapeDtypeStruct(x.shape, x....]
where the time goes in v2:
time: 46.7 us; the launch traced here: 46.5 us
  Pallas kernels  45.2 us (97%)
  between operations  1.29 us (3%)
    pallas_call x1, Pallas kernels, kernel_call(): pl.pallas_call(functools.partial(fused, sizes), out_shape=(jax.ShapeDtype...  43.8 us
    pallas_call x1, Pallas kernels, kernel_call(): pl.pallas_call(hand_on, out_shape=tuple((jax.ShapeDtypeStruct(x.shape, x....  1.38 us

profile of v2, /device:TPU:0, one launch (start us, length us, event | category | flops | bytes accessed | tf_op | source)
XLA Modules:
  0.0 46.5 jit_solution(9558653638857254764)
XLA Ops:
  1.3 43.8 %shard_map.131 = (bf16[32,448]{1,0:T(8,128)(2,1)}, bf16[4,1792]{1,0:T(4,128)(2,1)}) custom-call(bf16[32,256]{1,0:T(8,128)(2,1)} %bitcast.3, bf16[1536,4,256]{2,1,0:T(4,128)(2,1)} %k_hbm.1, bf16[1536,4,256]{2,1,0:T(4,128)(2,1)} %v_hbm.1, bf16[32,448]{1,0:T(8,128)(2,1)} %dec_hbm.1, bf16[448]{0:T(512)(128)(2,1)} %emb_hbm.1, bf16[448,2048]{1,0:T(8,128)(2,1)} %bitcast.2, ...), custom_call_target="tpu_custom_call" | custom-call | tf_op jit(solution)/shard_map/pallas_call | solution.py:654
  45.1 1.4 %shard_map.132 = (bf16[32,448]{1,0:T(8,128)(2,1)}, bf16[4,1792]{1,0:T(4,128)(2,1)}) custom-call(bf16[32,448]{1,0:T(8,128)(2,1)} %get-tuple-element.4.stream_in, bf16[4,1792]{1,0:T(4,128)(2,1)} %get-tuple-element.5.branch_in), custom_call_target="tpu_custom_call" | custom-call | tf_op jit(solution)/shard_map/pallas_call | solution.py:682
